TPU v7x, 128 devices: a whole 4x4x4 slice. The times are simulated.
128 devices in a mesh: tm: 16 (over y, z_lo, core), tensor: 8 (over z_hi, x).
Axes of the slice: x: 4, y: 4, z: 4 (z_hi: 2, z_lo: 2; z = z_hi * 2 + z_lo), core: 2. Of those that a mesh axis runs over, the one named last changes fastest.
Arguments:
- activations: bfloat16 [16384, 3072], P(('tm', 'tensor')), may hold values from -6 to 6
- mod_gain: float32 [3072], replicated, may hold values from 0.1 to 1.9
- mod_shift: float32 [3072], replicated, may hold values from -3 to 3
- out_gate: float32 [3072], replicated, may hold values from 0.5 to 2
- qkv_weight: bfloat16 [3072, 24, 384], P(None, 'tensor'), may hold values from -0.109375 to 0.109375
- out_weight: bfloat16 [24, 128, 3072], P('tensor'), may hold values from -0.109375 to 0.109375
- tile_mask: int32 [64, 7, 4, 4], P('tm'), may hold values 0 or 1
- cotangent: bfloat16 [16384, 3072], P('tm'), may hold values from -6 to 6
Outputs:
- layer_out: bfloat16 [16384, 3072], P(('tm', 'tensor'))
- input_grad: bfloat16 [16384, 3072], P(('tm', 'tensor'))
All inputs are finite; a program needn't handle non-finite values. No bound on the sum of `tile_mask` on one device may be relied on, other than what follows from the above.
Results may differ from a plain program's by a relative error of at most 0.015.
Values may be sent and summed in bfloat16 or wider, within the bound.
A program may use at most 320 MiB of HBM per device.

v0:
```python
import jax
import jax.numpy as jnp
from jax import lax
from jax.sharding import PartitionSpec as P

FRAME = 256
TILE = 64
RADIUS = 3
EPSILON = 1e-06


def extended(cells, sides, width):
    for axis, dim in sides:
        count = lax.axis_size(axis)
        ends = count - 1
        head = lax.slice_in_dim(cells, 0, width, axis=dim)
        tail = lax.slice_in_dim(cells, cells.shape[dim] - width, cells.shape[dim], axis=dim)
        cells = jnp.concatenate(
            [
                lax.ppermute(tail, axis, [(i, (i + 1) % count) for i in range(ends)]),
                cells,
                lax.ppermute(head, axis, [((i + 1) % count, i) for i in range(ends)]),
            ],
            axis=dim,
        )
    return cells


def norm_rows(inputs, mod_gain, mod_shift):
    floated = inputs.astype(jnp.float32)
    row_mean = jnp.mean(floated, axis=-1, keepdims=True)
    centered = floated - row_mean
    inverse = lax.rsqrt(jnp.mean(centered * centered, axis=-1, keepdims=True) + EPSILON)
    standard = centered * inverse
    return (standard, inverse, (standard * mod_gain + mod_shift).astype(jnp.bfloat16))


def norm_back(grad_norm, standard, inverse, mod_gain, cotangent):
    scaled_grad = grad_norm * mod_gain
    centered = scaled_grad - jnp.mean(scaled_grad, axis=-1, keepdims=True)
    projected = standard * jnp.mean(scaled_grad * standard, axis=-1, keepdims=True)
    return (cotangent.astype(jnp.float32) + inverse * (centered - projected)).astype(jnp.bfloat16)


def window_mask(tile_mask, first_frame, total_frames):
    expanded = jnp.repeat(jnp.repeat(tile_mask, TILE, axis=2), TILE, axis=3)
    frame_ids = lax.broadcasted_iota(jnp.int32, expanded.shape, 0) + first_frame
    offset_ids = lax.broadcasted_iota(jnp.int32, expanded.shape, 1)
    query_pos = lax.broadcasted_iota(jnp.int32, expanded.shape, 2)
    key_pos = lax.broadcasted_iota(jnp.int32, expanded.shape, 3)
    source = frame_ids + offset_ids - RADIUS
    diagonal = (offset_ids == RADIUS) & (query_pos // TILE == key_pos // TILE)
    inside = (source >= 0) & (source < total_frames)
    allowed = ((expanded == 1) | diagonal) & inside
    return jnp.transpose(allowed, (0, 2, 1, 3)).reshape(expanded.shape[0], expanded.shape[2], -1)


def window_rows(padded, frame_count, radius):
    stacked = jnp.stack(
        [padded[offset : offset + frame_count] for offset in range(2 * radius + 1)], axis=1
    )
    return stacked.reshape(frame_count, -1, padded.shape[2], padded.shape[3])


def spread_windows(window_grads, frame_count, radius):
    by_offset = window_grads.reshape(
        frame_count, 2 * radius + 1, -1, window_grads.shape[2], window_grads.shape[3]
    )
    summed = jnp.zeros((frame_count + 2 * radius,) + by_offset.shape[2:], jnp.float32)
    for offset in range(2 * radius + 1):
        summed = summed + jnp.pad(
            by_offset[:, offset], ((offset, 2 * radius - offset), (0, 0), (0, 0), (0, 0))
        )
    return summed


def attend(queries, window, allowed, score_scale):
    head_dim = queries.shape[-1]
    key_rows = window[..., :head_dim]
    value_rows = window[..., head_dim:]
    scores = (
        jnp.einsum("fqhc,fkhc->fhqk", queries, key_rows, preferred_element_type=jnp.float32)
        * score_scale
    )
    exponent = jnp.where(allowed[:, None], jnp.exp(scores), 0.0)
    totals = jnp.sum(exponent, axis=-1)
    numerator = jnp.einsum(
        "fhqk,fkhc->fqhc",
        exponent.astype(jnp.bfloat16),
        value_rows,
        preferred_element_type=jnp.float32,
    )
    output = (numerator / jnp.transpose(totals, (0, 2, 1))[..., None]).astype(jnp.bfloat16)
    return (output, totals)


def attend_back(queries, window, allowed, totals, output, grad_out, score_scale):
    head_dim = queries.shape[-1]
    key_rows = window[..., :head_dim]
    value_rows = window[..., head_dim:]
    scores = (
        jnp.einsum("fqhc,fkhc->fhqk", queries, key_rows, preferred_element_type=jnp.float32)
        * score_scale
    )
    probability = jnp.where(allowed[:, None], jnp.exp(scores), 0.0) / totals[..., None]
    grad_values = jnp.einsum(
        "fhqk,fqhc->fkhc",
        probability.astype(jnp.bfloat16),
        grad_out,
        preferred_element_type=jnp.float32,
    )
    grad_probs = jnp.einsum(
        "fqhc,fkhc->fhqk", grad_out, value_rows, preferred_element_type=jnp.float32
    )
    row_delta = jnp.einsum("fqhc,fqhc->fhq", grad_out, output, preferred_element_type=jnp.float32)
    grad_scores = (probability * (grad_probs - row_delta[..., None])).astype(jnp.bfloat16)
    grad_queries = jnp.einsum(
        "fhqk,fkhc->fqhc", grad_scores, key_rows, preferred_element_type=jnp.float32
    )
    grad_queries = (grad_queries * score_scale).astype(jnp.bfloat16)
    grad_keys = (
        jnp.einsum("fhqk,fqhc->fkhc", grad_scores, queries, preferred_element_type=jnp.float32)
        * score_scale
    )
    return (grad_queries, jnp.concatenate([grad_keys, grad_values], axis=-1))


def on_device(
    activations, mod_gain, mod_shift, out_gate, qkv_weight, out_weight, tile_mask, cotangent
):
    shard_rows = activations.shape[0]
    frame_count = tile_mask.shape[0]
    heads_here = qkv_weight.shape[1]
    head_dim = out_weight.shape[1]
    group_rows = frame_count * FRAME
    score_scale = head_dim ** (-0.5)
    standard, inverse, modulated = norm_rows(activations, mod_gain, mod_shift)
    joined_qkv = jnp.einsum(
        "rd,dhc->rhc",
        lax.all_gather(modulated, "tensor", axis=0, tiled=True),
        qkv_weight,
        preferred_element_type=jnp.float32,
    ).astype(jnp.bfloat16)
    joined_qkv = joined_qkv.reshape(frame_count, FRAME, heads_here, 3 * head_dim)
    queries = joined_qkv[..., :head_dim]
    padded = extended(joined_qkv[..., head_dim:], (("tm", 0),), RADIUS)
    first_frame = lax.axis_index("tm") * frame_count
    allowed = window_mask(tile_mask, first_frame, frame_count * lax.axis_size("tm"))
    window = window_rows(padded, frame_count, RADIUS)
    output, totals = attend(queries, window, allowed, score_scale)
    flat_out = output.reshape(group_rows, heads_here, head_dim)
    row_block = flat_out
    projection = lax.psum_scatter(
        jnp.einsum("rhc,hcd->rd", row_block, out_weight, preferred_element_type=jnp.float32).astype(
            jnp.bfloat16
        ),
        "tensor",
        scatter_dimension=0,
        tiled=True,
    ).astype(jnp.float32)
    layer_out = (activations.astype(jnp.float32) + out_gate * projection).astype(jnp.bfloat16)
    scaled = (cotangent.astype(jnp.float32) * out_gate).astype(jnp.bfloat16)
    grad_out = jnp.einsum("rd,hcd->rhc", scaled, out_weight, preferred_element_type=jnp.float32)
    grad_out = grad_out.astype(jnp.bfloat16).reshape(frame_count, FRAME, heads_here, head_dim)
    grad_queries, window_grads = attend_back(
        queries, window, allowed, totals, output, grad_out, score_scale
    )
    spread = spread_windows(window_grads, frame_count, RADIUS)
    rim_frames = jnp.concatenate([spread[:RADIUS], spread[frame_count + RADIUS :]], axis=0)
    arrived = extended(rim_frames.astype(jnp.bfloat16), (("tm", 0),), RADIUS).astype(
        rim_frames.dtype
    )
    own_part = spread[RADIUS : frame_count + RADIUS]
    from_below = jnp.pad(arrived[:RADIUS], ((0, frame_count - RADIUS), (0, 0), (0, 0), (0, 0)))
    from_above = jnp.pad(arrived[3 * RADIUS :], ((frame_count - RADIUS, 0), (0, 0), (0, 0), (0, 0)))
    grad_pairs = (own_part + from_below + from_above).astype(jnp.bfloat16)
    grad_joined = jnp.concatenate([grad_queries, grad_pairs], axis=-1).reshape(
        group_rows, heads_here, 3 * head_dim
    )
    row_block = grad_joined
    grad_norm = lax.psum_scatter(
        jnp.einsum("rhc,dhc->rd", row_block, qkv_weight, preferred_element_type=jnp.float32).astype(
            jnp.bfloat16
        ),
        "tensor",
        scatter_dimension=0,
        tiled=True,
    ).astype(jnp.float32)
    own_cotangent = lax.dynamic_slice_in_dim(
        cotangent, lax.axis_index("tensor") * shard_rows, shard_rows, 0
    )
    input_grad = norm_back(grad_norm, standard, inverse, mod_gain, own_cotangent)
    return (layer_out, input_grad)


def solution(mesh):
    placed = (
        P(("tm", "tensor"), None),
        P(),
        P(),
        P(),
        P(None, "tensor", None),
        P("tensor", None, None),
        P("tm", None, None, None),
        P("tm", None),
    )
    return jax.shard_map(
        on_device,
        mesh=mesh,
        in_specs=placed,
        out_specs=(P(("tm", "tensor"), None), P(("tm", "tensor"), None)),
        check_vma=False,
    )
```

profile of v0, /device:TPU:1, one launch (start us, length us, event | category | flops | bytes accessed | tf_op | source)
XLA Modules:
  0.0 538.4 jit_solution(2131804124469288829)
XLA Ops:
  7.2 1.5 convert_reduce_fusion
  8.7 1.5 fusion.50
  10.2 0.5 copy-done.16
  10.8 2.4 fusion.44
  13.7 0.8 eq.23
  14.4 91.4 %all-gather.2.cloned.1.call-done = bf16[1024,3072]{1,0:T(8,128)(2,1)} async-done(((bf16[128,3072]{1,0:T(8,128)(2,1)}), bf16[1024,3072]{1,0:T(8,128)(2,1)}) %all-gather.2.cloned.1.call-update) | async-done | bytes 6291472 | tf_op jit(solution)/shard_map/all_gather | solution.py:140
  105.8 12.4 %fusion.35 = bf16[1024,3,384]{2,0,1:T(8,128)(2,1)S(1)} fusion(bf16[3072,3,384]{2,0,1:T(8,128)(2,1)} %param.12, bf16[1024,3072]{1,0:T(8,128)(2,1)} %all-gather.2.cloned.1.call-done), kind=kOutput, calls=%fused_computation.60 | convolution fusion | flops 7248936960 | bytes 15728640 | tf_op jit(solution)/shard_map/rd,dhc->rhc/dot_general | solution.py:138
  118.3 1.8 fusion.93
  120.1 3.4 collective-permute-start
  123.5 6.3 %fusion.74 = bf16[1024,3,128]{2,0,1:T(8,128)(2,1)} fusion(bf16[3,128,3072]{2,1,0:T(8,128)(2,1)S(1)} %copy-done, bf16[1024,3072]{1,0:T(8,128)(2,1)} %param.15, f32[3072]{0:T(1024)S(1)} %copy-done.12), kind=kOutput, calls=%fused_computation.100 | convolution fusion | flops 2425749504 | bytes 9449472 | tf_op jit(solution)/shard_map/rd,hcd->rhc/dot_general | solution.py:163
  129.8 2.1 collective-permute-start.1
  132.0 4.6 fusion.15
  136.5 5.5 %copy.27 = pred[4,256,1792]{2,1,0:T(8,128)(4,1)} copy(pred[4,256,1792]{1,2,0:T(8,128)(4,1)} %bitcast.112) | data formatting | bytes 3670016 | tf_op jit(solution)/shard_map/jit(_where)/broadcast_in_dim | solution.py:85
  142.0 2.6 copy.50
  144.6 1.5 slice.112
  146.1 3.5 collective-permute-done
  149.6 1.4 fusion.63
  151.0 1.3 fusion.60
  152.3 1.3 fusion.67
  153.6 0.5 copy-done.3
  154.5 4.8 copy.25
  159.3 13.4 %fusion.1 = (f32[4,3,256]{2,1,0:T(4,128)S(1)}, f32[4,3,256,1792]{3,2,1,0:T(8,128)}) fusion(pred[4,256,1792]{2,1,0:T(8,128)(4,1)S(1)} %copy-done.6, bf16[4,1792,3,256]{3,1,2,0:T(8,128)(2,1)} %bitcast.108, bf16[4,256,3,384]{3,1,0,2:T(8,128)(2,1)S(1)} %bitcast.107), kind=kOutput, calls=%fused_computation.4 | convolution fusion | flops 1425798144 | bytes 30158848 | tf_op jit(solution)/shard_map/fqhc,fkhc->fhqk/dot_general | solution.py:82
  172.7 12.9 %fusion.22 = f32[4,1792,3,128]{1,3,2,0:T(8,128)} fusion(f32[4,3,256,1792]{3,2,1,0:T(8,128)} %get-tuple-element.20, f32[4,3,256]{2,1,0:T(4,128)S(1)} %get-tuple-element.19, pred[4,256,1792]{2,1,0:T(8,128)(4,1)S(1)} %copy-done.6, bf16[4,256,3,128]{3,1,0,2:T(8,128)(2,1)S(1)} %bitcast.116), kind=kOutput, calls=%fused_computation.30 | convolution fusion | flops 1431306240 | bytes 35663872 | tf_op jit(solution)/shard_map/fhqk,fqhc->fkhc/dot_general | solution.py:106
  185.6 13.6 %multiply_reduce_fusion = (f32[4,3,256]{2,1,0:T(4,128)S(1)}, bf16[4,256,3,128]{1,3,2,0:T(8,128)(2,1)}) fusion(f32[4,3,256,128]{2,3,1,0:T(8,128)} %copy.50, f32[4,256,3]{1,2,0:T(4,128)S(1)} %bitcast.120, f32[4,3,256,1792]{3,2,1,0:T(8,128)} %get-tuple-element.20, pred[4,256,1792]{2,1,0:T(8,128)(4,1)} %copy.27, bf16[4,1792,3,256]{3,1,2,0:T(8,128)(2,1)} %bitcast.109), kind=kOutput, calls=%fused_computation.96 | convolution fusion | flops 1427764224 | bytes 31744000 | tf_op jit(solution)/shard_map/fhqk,fkhc->fqhc/dot_general | solution.py:87
  199.2 17.3 %multiply_convert_fusion = bf16[4,3,256,1792]{3,2,1,0:T(8,128)(2,1)} fusion(f32[4,3,256]{2,1,0:T(4,128)S(1)} %get-tuple-element.21, bf16[4,1792,3,256]{3,1,2,0:T(8,128)(2,1)} %bitcast.110, f32[4,3,256]{2,1,0:T(4,128)S(1)} %get-tuple-element.19, f32[4,3,256,1792]{3,2,1,0:T(8,128)} %get-tuple-element.20, pred[4,256,1792]{2,1,0:T(8,128)(4,1)} %copy.27, ...), kind=kOutput, calls=%fused_computation.1 | convolution fusion | flops 1442316288 | bytes 41181184 | tf_op jit(solution)/shard_map/fqhc,fkhc->fhqk/dot_general | solution.py:112
  216.4 6.4 %multiply_bitcast_fusion = f32[4,1792,3,128]{1,3,2,0:T(8,128)S(1)} fusion(bf16[4,3,256,1792]{3,2,1,0:T(8,128)(2,1)} %multiply_convert_fusion, bf16[4,256,3,384]{3,1,0,2:T(8,128)(2,1)} %bitcast.105), kind=kOutput, calls=%fused_computation.12 | convolution fusion | flops 1412038656 | bytes 22806528 | tf_op jit(solution)/shard_map/fhqk,fqhc->fkhc/dot_general | solution.py:122
  222.8 1.1 copy-done.4
  223.9 7.7 %pad_maximum_fusion = f32[4,1792,3,256]{1,3,2,0:T(8,128)} fusion(f32[4,1792,3,128]{1,3,2,0:T(8,128)S(1)} %copy-done.4, f32[4,1792,3,128]{1,3,2,0:T(8,128)S(1)} %multiply_bitcast_fusion), kind=kLoop, calls=%fused_computation | loop fusion | flops 5505024 | bytes 44040192 | tf_op jit(solution)/shard_map/concatenate | solution.py:125
  231.6 21.7 %copy.35 = f32[4,1792,3,256]{3,1,2,0:T(8,128)} copy(f32[4,1792,3,256]{1,3,2,0:T(8,128)} %pad_maximum_fusion) | data formatting | bytes 44040192 | tf_op jit(solution)/shard_map/concatenate | solution.py:125
  253.3 14.5 %slice_bitcast_fusion.6 = (f32[4,256,3,256]{3,1,2,0:T(8,128)S(1)}, f32[4,256,3,256]{3,1,2,0:T(8,128)}, f32[4,256,3,256]{3,1,2,0:T(8,128)}, f32[4,256,3,256]{3,1,...) fusion(f32[4,7,256,3,256]{4,2,1,3,0:T(8,128)} %bitcast.102), kind=kLoop, calls=%fused_computation.51 | loop fusion | bytes 44040192 | tf_op jit(solution)/shard_map/squeeze | solution.py:72
  267.8 11.5 %fusion.91 = (bf16[10,256,3,256]{3,1,2,0:T(8,128)(2,1)}, f32[10,256,3,256]{3,1,2,0:T(8,128)}) fusion(f32[4,256,3,256]{3,1,2,0:T(8,128)} %get-tuple-element.11, f32[4,256,3,256]{3,1,2,0:T(8,128)} %get-tuple-element.12, f32[4,256,3,256]{3,1,2,0:T(8,128)} %get-tuple-element.7, f32[4,256,3,256]{3,1,2,0:T(8,128)} %get-tuple-element.8, ...), kind=kLoop, calls=%fused_computation.126 | loop fusion | flops 13762560 | bytes 33816576 | tf_op jit(solution)/shard_map/convert.2
  279.3 2.9 fusion.92
  282.2 4.4 collective-permute-start.2
  286.5 1.9 collective-permute-start.3
  288.5 10.4 %fusion.79 = bf16[4,256,3,128]{1,3,2,0:T(8,128)(2,1)} fusion(bf16[4,3,256,1792]{3,2,1,0:T(8,128)(2,1)} %multiply_convert_fusion, bf16[4,1792,3,256]{3,1,2,0:T(8,128)(2,1)} %bitcast.111), kind=kOutput, calls=%fused_computation.101 | convolution fusion | flops 1410072576 | bytes 17301504 | tf_op jit(solution)/shard_map/fhqk,fkhc->fqhc/dot_general | solution.py:117
  298.9 2.3 copy.42
  301.2 11.1 %collective-permute-done.2 = bf16[3,256,3,256]{3,1,2,0:T(8,128)(2,1)} collective-permute-done((bf16[3,256,3,256]{3,1,2,0:T(8,128)(2,1)S(1)}, bf16[3,256,3,256]{3,1,2,0:T(8,128)(2,1)}, u32[]{:S(2)}, u32[]{:S(2)}) %collective-permute-start.2) | collective-permute-done | bytes 1179680 | tf_op jit(solution)/shard_map/ppermute | solution.py:20
  312.3 1.6 fusion.82
  313.9 3.1 fusion.34
  317.1 0.3 pad_maximum_fusion.1
  317.7 10.1 %bitcast_convert_fusion = bf16[1024,3072]{1,0:T(8,128)(2,1)} fusion(bf16[1024,3,384]{2,0,1:T(8,128)(2,1)S(1)} %bitcast.113, bf16[3072,3,384]{2,0,1:T(8,128)(2,1)S(1)} %bitcast.119), kind=kOutput, calls=%fused_computation.6 | convolution fusion | flops 7250903040 | bytes 15728640 | tf_op jit(solution)/shard_map/rhc,dhc->rd/dot_general | solution.py:182
  327.9 1.1 copy-done.7
  329.0 1.2 copy.30
  330.1 6.6 %bitcast_convert_fusion.1 = bf16[1024,3072]{1,0:T(8,128)(2,1)} fusion(bf16[1024,3,128]{2,0,1:T(8,128)(2,1)} %bitcast.114, bf16[3,128,3072]{2,1,0:T(8,128)(2,1)S(1)} %copy-done), kind=kOutput, calls=%fused_computation.7 | convolution fusion | flops 2419064832 | bytes 9437184 | tf_op jit(solution)/shard_map/rhc,hcd->rd/dot_general | solution.py:154
  336.7 89.2 %reduce-scatter.5.cloned.1.call-done = bf16[128,3072]{1,0:T(8,128)(2,1)} async-done(((bf16[1024,3072]{1,0:T(8,128)(2,1)}), bf16[128,3072]{1,0:T(8,128)(2,1)}) %reduce-scatter.5.cloned.1.call-update) | async-done | bytes 786448 | tf_op jit(solution)/shard_map/reduce_scatter | solution.py:181
  426.0 1.6 fusion.69
  427.6 100.6 %reduce-scatter.3.cloned.1.call-done = bf16[128,3072]{1,0:T(8,128)(2,1)} async-done(((bf16[1024,3072]{1,0:T(8,128)(2,1)}), bf16[128,3072]{1,0:T(8,128)(2,1)}) %reduce-scatter.3.cloned.1.call-update) | async-done | bytes 786448 | tf_op jit(solution)/shard_map/reduce_scatter | solution.py:153
  528.2 3.7 fusion.49
  (63 shorter events, 1.4 us)
Async XLA Ops:
  7.2 116.3 %copy-start = (bf16[3,128,3072]{2,1,0:T(8,128)(2,1)S(1)}, bf16[3,128,3072]{2,1,0:T(8,128)(2,1)}, u32[]{:S(2)}) copy-start(bf16[3,128,3072]{2,1,0:T(8,128)(2,1)} %param.13) | copy-start | bytes 7077892
  7.2 6.1 %copy-start.11 = (s32[4,7,4,4]{1,3,2,0:T(4,128)S(1)}, s32[4,7,4,4]{1,3,2,0:T(4,128)}, u32[]{:S(2)}) copy-start(s32[4,7,4,4]{1,3,2,0:T(4,128)} %param.14) | copy-start | bytes 5380
  7.2 98.6 %all-gather.2.cloned.1.call-start = ((), (), s32[]{:S(2)}) async-start(), calls=%async_computation.2 | async-start | bytes 7077888 | tf_op jit(solution)/shard_map/all_gather | solution.py:140
  8.7 1.5 copy-start.14
  10.2 0.5 copy-start.16
  13.2 412.8 %reduce-scatter.5.cloned.1.call-start = ((), (), s32[]{:S(2)}) async-start(), calls=%async_computation.4 | async-start | bytes 7077888 | tf_op jit(solution)/shard_map/reduce_scatter | solution.py:181
  118.3 11.5 %copy-start.2 = (bf16[1024,3,384]{2,0,1:T(8,128)(2,1)}, bf16[1024,3,384]{2,0,1:T(8,128)(2,1)S(1)}, u32[]{:S(2)}) copy-start(bf16[1024,3,384]{2,0,1:T(8,128)(2,1)S(1)} %fusion.35) | copy-start | bytes 7077892
  118.3 5.2 copy-start.12
  120.1 11.8 %copy-start.9 = (pred[4,7,256,4]{2,3,1,0:T(4,128)(4,1)S(1)}, pred[4,7,256,4]{2,3,1,0:T(4,128)(4,1)}, u32[]{:S(2)}) copy-start(pred[4,7,256,4]{2,3,1,0:T(4,128)(4,1)} %eq.23) | copy-start | bytes 86020
  120.1 29.5 %collective-permute-start = (bf16[3,256,3,256]{3,1,0,2:T(8,128)(2,1)}, bf16[3,256,3,256]{3,1,0,2:T(8,128)(2,1)}, u32[]{:S(2)}, u32[]{:S(2)}) collective-permute-start(bf16[3,256,3,256]{3,1,0,2:T(8,128)(2,1)} %get-tuple-element.16), channel_id=1, source_target_pairs={{0,8},{8,16},{16,24},{24,32},{32,40},{40,48},{48,56},{56,64},{64,7... | collective-permute-start | bytes 3538952 | tf_op jit(solution)/shard_map/ppermute | solution.py:20
  129.8 24.4 %collective-permute-start.1 = (bf16[3,256,3,256]{3,1,0,2:T(8,128)(2,1)}, bf16[3,256,3,256]{3,1,0,2:T(8,128)(2,1)S(1)}, u32[]{:S(2)}, u32[]{:S(2)}) collective-permute-start(bf16[3,256,3,256]{3,1,0,2:T(8,128)(2,1)} %get-tuple-element.15), channel_id=1, source_target_pairs={{8,0},{16,8},{24,16},{32,24},{40,32},{48,40},{56,48},{64,56},{72,6... | collective-permute-start | bytes 3538952 | tf_op jit(solution)/shard_map/ppermute | solution.py:22
  152.2 1.8 copy-start.3
  154.5 4.8 copy-start.6
  159.3 13.4 %copy-start.8 = (bf16[1024,3,128]{2,0,1:T(8,128)(2,1)S(1)}, bf16[1024,3,128]{2,0,1:T(8,128)(2,1)}, u32[]{:S(2)}) copy-start(bf16[1024,3,128]{2,0,1:T(8,128)(2,1)} %fusion.74) | copy-start | bytes 2359300
  216.4 7.5 %copy-start.4 = (f32[4,1792,3,128]{1,3,2,0:T(8,128)S(1)}, f32[4,1792,3,128]{1,3,2,0:T(8,128)}, u32[]{:S(2)}) copy-start(f32[4,1792,3,128]{1,3,2,0:T(8,128)} %fusion.22) | copy-start | bytes 33030148
  282.2 30.2 %collective-permute-start.2 = (bf16[3,256,3,256]{3,1,2,0:T(8,128)(2,1)S(1)}, bf16[3,256,3,256]{3,1,2,0:T(8,128)(2,1)}, u32[]{:S(2)}, u32[]{:S(2)}) collective-permute-start(bf16[3,256,3,256]{3,1,2,0:T(8,128)(2,1)S(1)} %get-tuple-element.13), channel_id=1, source_target_pairs={{0,8},{8,16},{16,24},{24,32},{32,40},{40,48},{48,56},{56,64},{64,7... | collective-permute-start | bytes 3538952 | tf_op jit(solution)/shard_map/ppermute | solution.py:20
  286.5 25.8 %collective-permute-start.3 = (bf16[3,256,3,256]{3,1,2,0:T(8,128)(2,1)}, bf16[3,256,3,256]{3,1,2,0:T(8,128)(2,1)}, u32[]{:S(2)}, u32[]{:S(2)}) collective-permute-start(bf16[3,256,3,256]{3,1,2,0:T(8,128)(2,1)} %get-tuple-element.14), channel_id=1, source_target_pairs={{8,0},{16,8},{24,16},{32,24},{40,32},{48,40},{56,48},{64,56},{72,6... | collective-permute-start | bytes 3538952 | tf_op jit(solution)/shard_map/ppermute | solution.py:22
  301.2 12.7 %copy-start.18 = (pred[4]{0:T(512)(128)(4,1)S(1)}, pred[4]{0:T(512)(128)(4,1)}, u32[]{:S(2)}) copy-start(pred[4]{0:T(512)(128)(4,1)} %constant.71.clone.1) | copy-start | bytes 16
  312.3 5.4 slice-start
  313.9 3.2 copy-start.5
  313.9 3.8 slice-start.1
  327.8 1.1 copy-start.7
  327.8 200.3 %reduce-scatter.3.cloned.1.call-start = ((), (), s32[]{:S(2)}) async-start(), calls=%async_computation.3 | async-start | bytes 7077888 | tf_op jit(solution)/shard_map/reduce_scatter | solution.py:153
  336.7 89.3 %copy-start.1 = (bf16[128,3072]{1,0:T(8,128)(2,1)S(1)}, bf16[128,3072]{1,0:T(8,128)(2,1)}, u32[]{:S(2)}) copy-start(bf16[128,3072]{1,0:T(8,128)(2,1)} %param.8) | copy-start | bytes 2359300
  336.7 89.3 %copy-start.10 = (f32[3072]{0:T(1024)S(1)}, f32[3072]{0:T(1024)}, u32[]{:S(2)}) copy-start(f32[3072]{0:T(1024)} %param.9) | copy-start | bytes 36868
  336.7 89.3 %copy-start.15 = (f32[128]{0:T(128)S(1)}, f32[128]{0:T(128)}, u32[]{:S(2)}) copy-start(f32[128]{0:T(128)} %copy-done.14) | copy-start | bytes 1540
  336.7 89.3 %copy-start.17 = (f32[128]{0:T(128)S(1)}, f32[128]{0:T(128)}, u32[]{:S(2)}) copy-start(f32[128]{0:T(128)} %copy-done.16) | copy-start | bytes 1540
  336.7 191.5 %copy-start.13 = (f32[3072]{0:T(1024)S(1)}, f32[3072]{0:T(1024)}, u32[]{:S(2)}) copy-start(f32[3072]{0:T(1024)} %param.11) | copy-start | bytes 36868
Sparse Core Ops, SparseCore 0:
  13.3 92.4 all-gather.1
  328.0 97.9 reduce-scatter.4
  430.4 97.7 reduce-scatter.2
where the time goes:
time: 539 us; the launch traced here: 538 us
  waiting for transfers between devices  296 us (55%)
  matrix products  109 us (20%)
  local copies, waits for them, and re-layouts  63.4 us (12%)
  other arithmetic  43.8 us (8%)
  between operations  14.1 us (3%)
  starting transfers between devices  11.9 us (2%)
    reduce_scatter x1, waiting for transfers between devices, on_device(): lax.psum_scatter(jnp.einsum('rhc,hcd->rd', row_block, out_weight, preferr...  101 us
    all_gather x1, waiting for transfers between devices, on_device(): lax.all_gather(modulated, 'tensor', axis=0, tiled=True)  91.4 us
    reduce_scatter x1, waiting for transfers between devices, on_device(): lax.psum_scatter(jnp.einsum('rhc,dhc->rd', row_block, qkv_weight, preferr...  89.2 us
    concatenate x1, local copies, waits for them, and re-layouts, attend_back(): return (grad_queries, jnp.concatenate([grad_keys, grad_values], axis=-1))  21.7 us
    dot_general x1, matrix products, attend_back(): jnp.einsum('fqhc,fkhc->fhqk', grad_out, value_rows, preferred_element_typ...  17.3 us
    ppermute x2, waiting for transfers between devices, extended(): lax.ppermute(tail, axis, [(i, (i + 1) % count) for i in range(ends)])  14.6 us
    squeeze x1, local copies, waits for them, and re-layouts, spread_windows(): by_offset[:, offset]  14.5 us
    dot_general x1, matrix products, attend(): jnp.einsum('fhqk,fkhc->fqhc', exponent.astype(jnp.bfloat16), value_rows,...  13.6 us
  transfers between devices with their start and end apart: 7, of which 5 were waited for; matrix products, arithmetic and copies ran while one was open for 9% of the time, Pallas kernels for 0%

commit v1 on v0

--- a/solution.py
+++ b/solution.py
@@ -2,6 +2,7 @@
 import jax.numpy as jnp
 from jax import lax
 from jax.sharding import PartitionSpec as P
+from jax.lax import all_to_all, psum
 
 FRAME = 256
 TILE = 64
@@ -135,11 +136,18 @@
     group_rows = frame_count * FRAME
     score_scale = head_dim ** (-0.5)
     standard, inverse, modulated = norm_rows(activations, mod_gain, mod_shift)
+
+    def take_row_for(u):
+        frames = []
+        for _ in range(psum(1, "tensor")):
+            frames.append(u)
+        w_next = jnp.stack(frames)
+        row_out = all_to_all(w_next, "tensor", 0, 0)
+        view_out = jnp.concatenate(row_out, axis=0)
+        return view_out
+
     joined_qkv = jnp.einsum(
-        "rd,dhc->rhc",
-        lax.all_gather(modulated, "tensor", axis=0, tiled=True),
-        qkv_weight,
-        preferred_element_type=jnp.float32,
+        "rd,dhc->rhc", take_row_for(modulated), qkv_weight, preferred_element_type=jnp.float32
     ).astype(jnp.bfloat16)
     joined_qkv = joined_qkv.reshape(frame_count, FRAME, heads_here, 3 * head_dim)
     queries = joined_qkv[..., :head_dim]

time: 539 us -> 556 us (1.032)
  starting transfers between devices: 11.9 us -> 20.1 us
    all_gather x1 -> x0, waiting for transfers between devices: 91.4 us -> none  [on_device(): lax.all_gather(modulated, 'tensor', axis=0, tiled=True)]
    all_to_all x0 -> x1, waiting for transfers between devices: none -> 72.3 us  [take_row_for(): row_out = all_to_all(w_next, 'tensor', 0, 0)]
    reduce_scatter x1, waiting for transfers between devices: 89.2 us -> 113 us  [on_device(): lax.psum_scatter(jnp.einsum('rhc,dhc->rd', row_block, qkv_weight, preferr...]
    all_to_all x0 -> x1, starting transfers between devices: none -> 8.29 us  [take_row_for(): row_out = all_to_all(w_next, 'tensor', 0, 0)]
where the time goes in v1:
time: 556 us; the launch traced here: 555 us
  waiting for transfers between devices  301 us (54%)
  matrix products  109 us (20%)
  local copies, waits for them, and re-layouts  66.9 us (12%)
  other arithmetic  43 us (8%)
  starting transfers between devices  20.1 us (4%)
  between operations  14.4 us (3%)
    reduce_scatter x1, waiting for transfers between devices, on_device(): lax.psum_scatter(jnp.einsum('rhc,dhc->rd', row_block, qkv_weight, preferr...  113 us
    reduce_scatter x1, waiting for transfers between devices, on_device(): lax.psum_scatter(jnp.einsum('rhc,hcd->rd', row_block, out_weight, preferr...  101 us
    all_to_all x1, waiting for transfers between devices, take_row_for(): row_out = all_to_all(w_next, 'tensor', 0, 0)  72.3 us
    concatenate x1, local copies, waits for them, and re-layouts, attend_back(): return (grad_queries, jnp.concatenate([grad_keys, grad_values], axis=-1))  21.8 us
    dot_general x1, matrix products, attend_back(): jnp.einsum('fqhc,fkhc->fhqk', grad_out, value_rows, preferred_element_typ...  17.3 us
    ppermute x2, waiting for transfers between devices, extended(): lax.ppermute(tail, axis, [(i, (i + 1) % count) for i in range(ends)])  14.7 us
    squeeze x1, local copies, waits for them, and re-layouts, spread_windows(): by_offset[:, offset]  14.5 us
    dot_general x1, matrix products, attend(): jnp.einsum('fhqk,fkhc->fqhc', exponent.astype(jnp.bfloat16), value_rows,...  13.6 us
  transfers between devices with their start and end apart: 7, of which 5 were waited for; matrix products, arithmetic and copies ran while one was open for 9% of the time, Pallas kernels for 0%

profile of v1, /device:TPU:1, one launch (start us, length us, event | category | flops | bytes accessed | tf_op | source)
XLA Modules:
  0.0 554.7 jit_solution(9279968688472972569)
XLA Ops:
  7.2 1.5 convert_reduce_fusion
  8.7 1.5 fusion.45
  10.2 0.5 copy-done.16
  10.7 1.5 fusion.39
  12.2 3.4 stack.35
  15.7 8.3 %all-to-all-start = ((bf16[8,128,3072]{2,1,0:T(8,128)(2,1)}), bf16[8,128,3072]{2,1,0:T(8,128)(2,1)}, u32[]{:S(2)}, u32[]{:S(2)}) async-start(bf16[8,128,3072]{2,1,0:T(8,128)(2,1)} %stack.35), calls=%async_computation | async-start | bytes 12582912 | tf_op jit(solution)/shard_map/all_to_all | solution.py:145
  24.4 0.8 eq.23
  25.2 72.3 %all-to-all-done = bf16[8,128,3072]{2,1,0:T(8,128)(2,1)} async-done(((bf16[8,128,3072]{2,1,0:T(8,128)(2,1)}), bf16[8,128,3072]{2,1,0:T(8,128)(2,1)}, u32[]{:S(2)}, u32[]{:S(2)}) %all-to-all-start) | async-done | bytes 6291488 | tf_op jit(solution)/shard_map/all_to_all | solution.py:145
  97.5 12.4 %convolution_convert_fusion = bf16[1024,3,384]{2,0,1:T(8,128)(2,1)S(1)} fusion(bf16[1024,3072,1]{1,0,2:T(8,128)(2,1)} %bitcast.3, bf16[3072,3,384]{2,0,1:T(8,128)(2,1)} %param.12), kind=kOutput, calls=%fused_computation.58 | convolution fusion | flops 7248936960 | bytes 15728640 | tf_op jit(solution)/shard_map/rd,dhc->rhc/dot_general | solution.py:149
  110.0 1.8 fusion.88
  111.9 3.5 collective-permute-start
  115.4 6.3 %fusion.69 = bf16[1024,3,128]{2,0,1:T(8,128)(2,1)} fusion(bf16[3,128,3072]{2,1,0:T(8,128)(2,1)S(1)} %copy-done, bf16[1024,3072]{1,0:T(8,128)(2,1)} %param.15, f32[3072]{0:T(1024)S(1)} %copy-done.12), kind=kOutput, calls=%fused_computation.98 | convolution fusion | flops 2425749504 | bytes 9449472 | tf_op jit(solution)/shard_map/rd,hcd->rhc/dot_general | solution.py:171
  121.7 2.0 collective-permute-start.1
  123.7 4.6 fusion.15
  128.3 5.4 copy.27
  133.8 2.6 copy.50
  136.3 1.5 slice.112
  137.8 3.6 collective-permute-done
  141.4 1.4 fusion.58
  142.8 1.3 fusion.55
  144.1 1.3 fusion.62
  146.4 4.8 copy.25
  151.2 13.3 %fusion.1 = (f32[4,3,256]{2,1,0:T(4,128)S(1)}, f32[4,3,256,1792]{3,2,1,0:T(8,128)}) fusion(pred[4,256,1792]{2,1,0:T(8,128)(4,1)S(1)} %copy-done.6, bf16[4,1792,3,256]{3,1,2,0:T(8,128)(2,1)} %bitcast.107, bf16[4,256,3,384]{3,1,0,2:T(8,128)(2,1)S(1)} %bitcast.106), kind=kOutput, calls=%fused_computation.4 | convolution fusion | flops 1425798144 | bytes 30158848 | tf_op jit(solution)/shard_map/fqhc,fkhc->fhqk/dot_general | solution.py:83
  164.5 12.9 %fusion.20 = f32[4,1792,3,128]{1,3,2,0:T(8,128)} fusion(f32[4,3,256,1792]{3,2,1,0:T(8,128)} %get-tuple-element.20, f32[4,3,256]{2,1,0:T(4,128)S(1)} %get-tuple-element.19, pred[4,256,1792]{2,1,0:T(8,128)(4,1)S(1)} %copy-done.6, bf16[4,256,3,128]{3,1,0,2:T(8,128)(2,1)S(1)} %bitcast.115), kind=kOutput, calls=%fused_computation.28 | convolution fusion | flops 1431306240 | bytes 35663872 | tf_op jit(solution)/shard_map/fhqk,fqhc->fkhc/dot_general | solution.py:107
  177.4 13.6 %multiply_reduce_fusion = (f32[4,3,256]{2,1,0:T(4,128)S(1)}, bf16[4,256,3,128]{1,3,2,0:T(8,128)(2,1)}) fusion(f32[4,3,256,128]{2,3,1,0:T(8,128)} %copy.50, f32[4,256,3]{1,2,0:T(4,128)S(1)} %bitcast.119, f32[4,3,256,1792]{3,2,1,0:T(8,128)} %get-tuple-element.20, pred[4,256,1792]{2,1,0:T(8,128)(4,1)} %copy.27, bf16[4,1792,3,256]{3,1,2,0:T(8,128)(2,1)} %bitcast.108), kind=kOutput, calls=%fused_computation.94 | convolution fusion | flops 1427764224 | bytes 31744000 | tf_op jit(solution)/shard_map/fhqk,fkhc->fqhc/dot_general | solution.py:88
  191.0 17.3 %multiply_convert_fusion = bf16[4,3,256,1792]{3,2,1,0:T(8,128)(2,1)} fusion(f32[4,3,256]{2,1,0:T(4,128)S(1)} %get-tuple-element.21, bf16[4,1792,3,256]{3,1,2,0:T(8,128)(2,1)} %bitcast.109, f32[4,3,256]{2,1,0:T(4,128)S(1)} %get-tuple-element.19, f32[4,3,256,1792]{3,2,1,0:T(8,128)} %get-tuple-element.20, pred[4,256,1792]{2,1,0:T(8,128)(4,1)} %copy.27, ...), kind=kOutput, calls=%fused_computation.1 | convolution fusion | flops 1442316288 | bytes 41181184 | tf_op jit(solution)/shard_map/fqhc,fkhc->fhqk/dot_general | solution.py:113
  208.3 6.4 %multiply_bitcast_fusion = f32[4,1792,3,128]{1,3,2,0:T(8,128)S(1)} fusion(bf16[4,3,256,1792]{3,2,1,0:T(8,128)(2,1)} %multiply_convert_fusion, bf16[4,256,3,384]{3,1,0,2:T(8,128)(2,1)} %bitcast.104), kind=kOutput, calls=%fused_computation.12 | convolution fusion | flops 1412038656 | bytes 22806528 | tf_op jit(solution)/shard_map/fhqk,fqhc->fkhc/dot_general | solution.py:123
  214.7 1.1 copy-done.4
  215.8 7.7 %pad_maximum_fusion = f32[4,1792,3,256]{1,3,2,0:T(8,128)} fusion(f32[4,1792,3,128]{1,3,2,0:T(8,128)S(1)} %copy-done.4, f32[4,1792,3,128]{1,3,2,0:T(8,128)S(1)} %multiply_bitcast_fusion), kind=kLoop, calls=%fused_computation | loop fusion | flops 5505024 | bytes 44040192 | tf_op jit(solution)/shard_map/concatenate | solution.py:126
  223.5 21.8 %copy.35 = f32[4,1792,3,256]{3,1,2,0:T(8,128)} copy(f32[4,1792,3,256]{1,3,2,0:T(8,128)} %pad_maximum_fusion) | data formatting | bytes 44040192 | tf_op jit(solution)/shard_map/concatenate | solution.py:126
  245.2 14.5 %slice_bitcast_fusion.6 = (f32[4,256,3,256]{3,1,2,0:T(8,128)S(1)}, f32[4,256,3,256]{3,1,2,0:T(8,128)}, f32[4,256,3,256]{3,1,2,0:T(8,128)}, f32[4,256,3,256]{3,1,...) fusion(f32[4,7,256,3,256]{4,2,1,3,0:T(8,128)} %bitcast.101), kind=kLoop, calls=%fused_computation.49 | loop fusion | bytes 44040192 | tf_op jit(solution)/shard_map/squeeze | solution.py:73
  259.7 11.5 %fusion.86 = (bf16[10,256,3,256]{3,1,2,0:T(8,128)(2,1)}, f32[10,256,3,256]{3,1,2,0:T(8,128)}) fusion(f32[4,256,3,256]{3,1,2,0:T(8,128)} %get-tuple-element.11, f32[4,256,3,256]{3,1,2,0:T(8,128)} %get-tuple-element.12, f32[4,256,3,256]{3,1,2,0:T(8,128)} %get-tuple-element.7, f32[4,256,3,256]{3,1,2,0:T(8,128)} %get-tuple-element.8, ...), kind=kLoop, calls=%fused_computation.124 | loop fusion | flops 13762560 | bytes 33816576 | tf_op jit(solution)/shard_map/convert.2
  271.2 2.9 fusion.87
  274.1 4.4 collective-permute-start.2
  278.5 1.9 collective-permute-start.3
  280.4 10.4 %fusion.74 = bf16[4,256,3,128]{1,3,2,0:T(8,128)(2,1)} fusion(bf16[4,3,256,1792]{3,2,1,0:T(8,128)(2,1)} %multiply_convert_fusion, bf16[4,1792,3,256]{3,1,2,0:T(8,128)(2,1)} %bitcast.110), kind=kOutput, calls=%fused_computation.99 | convolution fusion | flops 1410072576 | bytes 17301504 | tf_op jit(solution)/shard_map/fhqk,fkhc->fqhc/dot_general | solution.py:118
  290.8 2.3 copy.42
  293.1 11.1 %collective-permute-done.2 = bf16[3,256,3,256]{3,1,2,0:T(8,128)(2,1)} collective-permute-done((bf16[3,256,3,256]{3,1,2,0:T(8,128)(2,1)S(1)}, bf16[3,256,3,256]{3,1,2,0:T(8,128)(2,1)}, u32[]{:S(2)}, u32[]{:S(2)}) %collective-permute-start.2) | collective-permute-done | bytes 1179680 | tf_op jit(solution)/shard_map/ppermute | solution.py:21
  304.2 1.6 fusion.77
  305.9 3.1 fusion.32
  309.6 10.1 %bitcast_convert_fusion = bf16[1024,3072]{1,0:T(8,128)(2,1)} fusion(bf16[1024,3,384]{2,0,1:T(8,128)(2,1)S(1)} %bitcast.112, bf16[3072,3,384]{2,0,1:T(8,128)(2,1)S(1)} %bitcast.118), kind=kOutput, calls=%fused_computation.6 | convolution fusion | flops 7250903040 | bytes 15728640 | tf_op jit(solution)/shard_map/rhc,dhc->rd/dot_general | solution.py:190
  319.8 1.1 copy-done.7
  320.9 1.2 copy.30
  322.0 6.5 %bitcast_convert_fusion.1 = bf16[1024,3072]{1,0:T(8,128)(2,1)} fusion(bf16[1024,3,128]{2,0,1:T(8,128)(2,1)} %bitcast.113, bf16[3,128,3072]{2,1,0:T(8,128)(2,1)S(1)} %copy-done), kind=kOutput, calls=%fused_computation.7 | convolution fusion | flops 2419064832 | bytes 9437184 | tf_op jit(solution)/shard_map/rhc,hcd->rd/dot_general | solution.py:162
  328.6 112.8 %reduce-scatter.5.cloned.1.call-done = bf16[128,3072]{1,0:T(8,128)(2,1)} async-done(((bf16[1024,3072]{1,0:T(8,128)(2,1)}), bf16[128,3072]{1,0:T(8,128)(2,1)}) %reduce-scatter.5.cloned.1.call-update) | async-done | bytes 786448 | tf_op jit(solution)/shard_map/reduce_scatter | solution.py:189
  441.4 1.6 fusion.64
  443.0 101.1 %reduce-scatter.3.cloned.1.call-done = bf16[128,3072]{1,0:T(8,128)(2,1)} async-done(((bf16[1024,3072]{1,0:T(8,128)(2,1)}), bf16[128,3072]{1,0:T(8,128)(2,1)}) %reduce-scatter.3.cloned.1.call-update) | async-done | bytes 786448 | tf_op jit(solution)/shard_map/reduce_scatter | solution.py:161
  544.2 3.7 fusion.44
  (63 shorter events, 2.2 us)
Async XLA Ops:
  7.2 108.2 %copy-start = (bf16[3,128,3072]{2,1,0:T(8,128)(2,1)S(1)}, bf16[3,128,3072]{2,1,0:T(8,128)(2,1)}, u32[]{:S(2)}) copy-start(bf16[3,128,3072]{2,1,0:T(8,128)(2,1)} %param.13) | copy-start | bytes 7077892
  8.7 1.5 copy-start.14
  10.2 0.5 copy-start.16
  15.7 8.3 %copy-start.11 = (s32[4,7,4,4]{1,3,2,0:T(4,128)S(1)}, s32[4,7,4,4]{1,3,2,0:T(4,128)}, u32[]{:S(2)}) copy-start(s32[4,7,4,4]{1,3,2,0:T(4,128)} %param.14) | copy-start | bytes 5380
  15.7 81.9 %all-to-all-start = ((bf16[8,128,3072]{2,1,0:T(8,128)(2,1)}), bf16[8,128,3072]{2,1,0:T(8,128)(2,1)}, u32[]{:S(2)}, u32[]{:S(2)}) async-start(bf16[8,128,3072]{2,1,0:T(8,128)(2,1)} %stack.35), calls=%async_computation | async-start | bytes 12582912 | tf_op jit(solution)/shard_map/all_to_all | solution.py:145
  23.9 417.4 %reduce-scatter.5.cloned.1.call-start = ((), (), s32[]{:S(2)}) async-start(), calls=%async_computation.4 | async-start | bytes 7077888 | tf_op jit(solution)/shard_map/reduce_scatter | solution.py:189
  110.0 11.7 %copy-start.2 = (bf16[1024,3,384]{2,0,1:T(8,128)(2,1)}, bf16[1024,3,384]{2,0,1:T(8,128)(2,1)S(1)}, u32[]{:S(2)}) copy-start(bf16[1024,3,384]{2,0,1:T(8,128)(2,1)S(1)} %convolution_convert_fusion) | copy-start | bytes 7077892
  110.0 5.4 copy-start.12
  111.9 11.8 %copy-start.9 = (pred[4,7,256,4]{2,3,1,0:T(4,128)(4,1)S(1)}, pred[4,7,256,4]{2,3,1,0:T(4,128)(4,1)}, u32[]{:S(2)}) copy-start(pred[4,7,256,4]{2,3,1,0:T(4,128)(4,1)} %eq.23) | copy-start | bytes 86020
  111.9 29.6 %collective-permute-start = (bf16[3,256,3,256]{3,1,0,2:T(8,128)(2,1)}, bf16[3,256,3,256]{3,1,0,2:T(8,128)(2,1)}, u32[]{:S(2)}, u32[]{:S(2)}) collective-permute-start(bf16[3,256,3,256]{3,1,0,2:T(8,128)(2,1)} %get-tuple-element.16), channel_id=1, source_target_pairs={{0,8},{8,16},{16,24},{24,32},{32,40},{40,48},{48,56},{56,64},{64,7... | collective-permute-start | bytes 3538952 | tf_op jit(solution)/shard_map/ppermute | solution.py:21
  121.7 24.4 %collective-permute-start.1 = (bf16[3,256,3,256]{3,1,0,2:T(8,128)(2,1)}, bf16[3,256,3,256]{3,1,0,2:T(8,128)(2,1)S(1)}, u32[]{:S(2)}, u32[]{:S(2)}) collective-permute-start(bf16[3,256,3,256]{3,1,0,2:T(8,128)(2,1)} %get-tuple-element.15), channel_id=1, source_target_pairs={{8,0},{16,8},{24,16},{32,24},{40,32},{48,40},{56,48},{64,56},{72,6... | collective-permute-start | bytes 3538952 | tf_op jit(solution)/shard_map/ppermute | solution.py:23
  144.1 1.8 copy-start.3
  146.4 4.8 copy-start.6
  151.2 13.3 %copy-start.8 = (bf16[1024,3,128]{2,0,1:T(8,128)(2,1)S(1)}, bf16[1024,3,128]{2,0,1:T(8,128)(2,1)}, u32[]{:S(2)}) copy-start(bf16[1024,3,128]{2,0,1:T(8,128)(2,1)} %fusion.69) | copy-start | bytes 2359300
  208.3 7.5 %copy-start.4 = (f32[4,1792,3,128]{1,3,2,0:T(8,128)S(1)}, f32[4,1792,3,128]{1,3,2,0:T(8,128)}, u32[]{:S(2)}) copy-start(f32[4,1792,3,128]{1,3,2,0:T(8,128)} %fusion.20) | copy-start | bytes 33030148
  274.1 30.2 %collective-permute-start.2 = (bf16[3,256,3,256]{3,1,2,0:T(8,128)(2,1)S(1)}, bf16[3,256,3,256]{3,1,2,0:T(8,128)(2,1)}, u32[]{:S(2)}, u32[]{:S(2)}) collective-permute-start(bf16[3,256,3,256]{3,1,2,0:T(8,128)(2,1)S(1)} %get-tuple-element.13), channel_id=1, source_target_pairs={{0,8},{8,16},{16,24},{24,32},{32,40},{40,48},{48,56},{56,64},{64,7... | collective-permute-start | bytes 3538952 | tf_op jit(solution)/shard_map/ppermute | solution.py:21
  278.5 25.8 %collective-permute-start.3 = (bf16[3,256,3,256]{3,1,2,0:T(8,128)(2,1)}, bf16[3,256,3,256]{3,1,2,0:T(8,128)(2,1)}, u32[]{:S(2)}, u32[]{:S(2)}) collective-permute-start(bf16[3,256,3,256]{3,1,2,0:T(8,128)(2,1)} %get-tuple-element.14), channel_id=1, source_target_pairs={{8,0},{16,8},{24,16},{32,24},{40,32},{48,40},{56,48},{64,56},{72,6... | collective-permute-start | bytes 3538952 | tf_op jit(solution)/shard_map/ppermute | solution.py:23
  293.1 12.7 %copy-start.18 = (pred[4]{0:T(512)(128)(4,1)S(1)}, pred[4]{0:T(512)(128)(4,1)}, u32[]{:S(2)}) copy-start(pred[4]{0:T(512)(128)(4,1)} %constant.71.clone.1) | copy-start | bytes 16
  304.2 5.4 slice-start
  305.8 3.2 copy-start.5
  305.8 3.8 slice-start.1
  319.8 1.1 copy-start.7
  319.8 224.4 %reduce-scatter.3.cloned.1.call-start = ((), (), s32[]{:S(2)}) async-start(), calls=%async_computation.3 | async-start | bytes 7077888 | tf_op jit(solution)/shard_map/reduce_scatter | solution.py:161
  328.5 112.8 %copy-start.1 = (bf16[128,3072]{1,0:T(8,128)(2,1)S(1)}, bf16[128,3072]{1,0:T(8,128)(2,1)}, u32[]{:S(2)}) copy-start(bf16[128,3072]{1,0:T(8,128)(2,1)} %param.8) | copy-start | bytes 2359300
  328.5 112.8 %copy-start.10 = (f32[3072]{0:T(1024)S(1)}, f32[3072]{0:T(1024)}, u32[]{:S(2)}) copy-start(f32[3072]{0:T(1024)} %param.9) | copy-start | bytes 36868
  328.5 112.9 %copy-start.15 = (f32[128]{0:T(128)S(1)}, f32[128]{0:T(128)}, u32[]{:S(2)}) copy-start(f32[128]{0:T(128)} %copy-done.14) | copy-start | bytes 1540
  328.5 112.9 %copy-start.17 = (f32[128]{0:T(128)S(1)}, f32[128]{0:T(128)}, u32[]{:S(2)}) copy-start(f32[128]{0:T(128)} %copy-done.16) | copy-start | bytes 1540
  328.5 215.6 %copy-start.13 = (f32[3072]{0:T(1024)S(1)}, f32[3072]{0:T(1024)}, u32[]{:S(2)}) copy-start(f32[3072]{0:T(1024)} %param.11) | copy-start | bytes 36868
Sparse Core Ops, SparseCore 0:
  319.9 121.4 reduce-scatter.4
  445.8 98.3 reduce-scatter.2
